TPU v7x, 32 devices: a whole 2x2x4 slice. The times are simulated.
32 devices in a mesh: leaf: 2 (over y), row: 4 (over x, core), col: 4 (over z).
Axes of the slice: x: 2, y: 2, z: 4, core: 2. Of those that a mesh axis runs over, the one named last changes fastest.
Arguments:
- panel: float32 [8192, 1024], P(('leaf', 'row'), 'col'), may hold values from -1.2 to 1.2
- block_mask: int32 [64, 8], P(('leaf', 'row'), 'col'), may hold values 0 or 1
- front_rest: float32 [4096, 4096], P(('leaf', 'row'), 'col'), may hold values from -6 to 6
- row_maps: int32 [8, 4], P(('leaf', 'row')), may hold values from 0 to 3, each once within a row
- col_maps: int32 [8, 12], P(('leaf', 'col')), may hold values from 0 to 11, each once within a row
Outputs:
- parent: float32 [2048, 6144], P(('leaf', 'row'), 'col')
Inputs may be any that keep to these rules, and one draw needn't show every extreme that they name: `row_maps`: each row is a permutation of 0 to 3. `col_maps`: each row is a permutation of 0 to 11; only its first 8 entries are used.
All inputs are finite; a program needn't handle non-finite values. No bound on the sum of `block_mask` on one device may be relied on, other than what follows from the above.
Results may differ from a plain program's by a relative error of at most 0.0003.
Values sent between devices are 32-bit elements; how exact they have to be, the bound alone decides.
A program may use at most 64 MiB of HBM per device.

v0:
```python
import functools

import jax
import jax.numpy as jnp
from jax import lax
from jax.experimental import pallas as pl
from jax.experimental.pallas import tpu as pltpu
from jax.sharding import PartitionSpec as P

BLK = 128
PC = 6144
F32 = jnp.float32
BF16 = jnp.bfloat16


def split(value):
    high = value.astype(BF16)
    return high, (value - high.astype(F32)).astype(BF16)


def update_kernel(
    n_leaf, n_row, n_col,
    pick_ref, flag_ref, cols_ref, panel_ref, front_hbm,
    mine_ref, got_ref, other_ref,
    p_ref, relay, win, col, a_cat, b_cat, front, front_sorted, snd,
    win_send, win_recv, rel_send, rel_recv, s1_send, col_recv, s2_send, fwd_send,
    sib_send, sib_recv, loc_sem, self_sem, map_send, map_recv,
):
    leaf, r, c = lax.axis_index("leaf"), lax.axis_index("row"), lax.axis_index("col")
    x, k = r // 2, r % 2
    sib = lax.rem(leaf + n_leaf // 2, n_leaf)
    upper = leaf // (n_leaf // 2) % 2
    keep, width = win.shape[2], win.shape[3]
    win_rows = 2 * keep
    win_blocks = win_rows // BLK
    subs = col.shape[0]
    quarter = p_ref.shape[0] // n_row
    depth = n_col * width

    def remote(src, dst, ssem, rsem, row=None, column=None, other_leaf=None):
        where = {
            "leaf": leaf if other_leaf is None else other_leaf,
            "row": r if row is None else row,
            "col": c if column is None else column,
        }
        return pltpu.make_async_remote_copy(
            src_ref=src, dst_ref=dst, send_sem=ssem, recv_sem=rsem,
            device_id=where, device_id_type=pl.DeviceIdType.MESH,
        )

    x_row, pair_row = (1 - x) * 2 + k, x * 2 + 1 - k

    front_copy = pltpu.make_async_copy(front_hbm, front, loc_sem.at[0])
    front_copy.start()
    first_kept = upper * (win_blocks // 2)
    first_sent = (1 - upper) * (win_blocks // 2)
    parent_at = [first_sent + i for i in range(win_blocks // 2)]
    parent_at += [first_kept + i for i in range(win_blocks // 2)]

    def picked(block_of, index, lanes):
        total = None
        for j in range(win_blocks):
            term = block_of(j) * pick_ref[parent_at[index] * win_blocks + j][:, :lanes]
            total = term if total is None else total + term
        return total

    for i in range(p_ref.shape[0] // BLK):
        for b in range(p_ref.shape[1] // BLK):
            spot = slice(i * BLK, (i + 1) * BLK), slice(b * BLK, (b + 1) * BLK)
            flag = flag_ref[i:i + 1, b:b + 1].astype(F32)
            p_ref[spot] = panel_ref[spot] * jnp.broadcast_to(flag, (BLK, BLK))

    for i in range(win_blocks):
        win[i * BLK // keep, c, pl.ds(i * BLK % keep, BLK), :] = picked(
            lambda j: p_ref[j * BLK:(j + 1) * BLK, :], i, p_ref.shape[1]
        )

    barrier = pltpu.get_barrier_semaphore()

    def greet(row, column, other_leaf):
        pl.semaphore_signal(
            barrier, inc=1, device_id={"leaf": other_leaf, "row": row, "col": column},
            device_id_type=pl.DeviceIdType.MESH,
        )

    for step in range(1, n_col):
        for kk in range(2):
            greet(x * 2 + kk, lax.rem(c + step, n_col), leaf)
    greet(pair_row, c, leaf)
    greet(x_row, c, leaf)
    greet(r, c, sib)
    pl.semaphore_wait(barrier, 2 * (n_col - 1) + 3)

    def pass_window(part, owner, side):
        piece = win.at[part, owner]
        return remote(
            piece, piece, win_send.at[part, side, owner], win_recv.at[part, owner],
            column=c + 1 if side == 0 else c - 1,
        )

    def has(side):
        return c + 1 < n_col if side == 0 else c >= 1

    def send_window(part):
        for side in range(2):
            @pl.when(has(side))
            def _():
                pass_window(part, c, side).start()

    other_cols = remote(cols_ref, other_ref, map_send.at[0], map_recv.at[0], other_leaf=sib)
    other_cols.start()
    send_window(0)
    half = 2 * quarter
    to_relay = remote(
        p_ref.at[pl.ds(pl.multiple_of((1 - x) * half, half), half)], relay,
        rel_send.at[0], rel_recv.at[0], row=x_row,
    )
    to_relay.start()

    def from_left(d):
        return c - d >= 0

    def from_right(d):
        return c + d < n_col

    def take_window(part, d, side, forward):
        owner = c - d if side == 0 else c + d

        @pl.when(from_left(d) if side == 0 else from_right(d))
        def _():
            pass_window(part, owner, side).wait_recv()
            if forward:
                @pl.when(has(side))
                def _():
                    pass_window(part, owner, side).start()

    def relay_window(part):
        for d in range(1, n_col - 1):
            for side in range(2):
                take_window(part, d, side, True)

    relay_window(0)

    to_relay.wait_recv()

    def scatter(sub, own, kk):
        target = x * 2 + k if own else (1 - x) * 2 + k
        q = x * 2 + kk
        if own:
            start = pl.multiple_of(q * quarter + sub * BLK, BLK)
            src = p_ref.at[pl.ds(start, BLK)]
        else:
            src = relay.at[pl.ds(kk * quarter + sub * BLK, BLK)]
        dst = col.at[sub, c, pl.ds(pl.multiple_of(q * BLK, BLK), BLK)]
        slot = s1_send.at[sub, int(own), kk]
        here = jnp.logical_and(target == c, k == kk)
        away = remote(src, dst, slot, col_recv.at[sub, q, c], row=q, column=target)
        stay = pltpu.make_async_copy(src, dst, self_sem.at[sub])
        return here, away, stay

    def at_end(own):
        target = x * 2 + k if own else (1 - x) * 2 + k
        return jnp.logical_or(target == 0, target == n_col - 1)

    def send_quarters(sub, own, kk):
        here, away, stay = scatter(sub, own, kk)

        @pl.when(here)
        def _():
            stay.start()

        @pl.when(jnp.logical_not(here))
        def _():
            away.start()

    for sub in range(subs):
        for last in (True, False):
            for own in (True, False):
                @pl.when(at_end(own) if last else jnp.logical_not(at_end(own)))
                def _():
                    for kk in range(2):
                        send_quarters(sub, own, kk)

    send_window(1)

    def slot_of(sub, q, owner):
        return col.at[sub, owner, pl.ds(pl.multiple_of(q * BLK, BLK), BLK)]

    def hand_on(sub, q, owner, ssem, row):
        part = slot_of(sub, q, owner)
        return remote(part, part, ssem, col_recv.at[sub, q, owner], row=row)

    steps = [0]
    for d in range(1, n_col):
        steps += [-d, d]

    def each(offset, run):
        owner = c + offset
        if offset == 0:
            run(owner)
        else:
            @pl.when(from_left(-offset) if offset < 0 else from_right(offset))
            def _():
                run(owner)

    def arrive(sub, q, owner):
        hand_on(sub, q, owner, s2_send.at[sub, owner, 0], pair_row).wait_recv()

    is_source = k == c % 2

    def own_piece_at(sub, offset):
        def run(owner):
            if offset == 0:
                @pl.when(is_source)
                def _():
                    pltpu.make_async_copy(
                        slot_of(sub, r, owner), slot_of(sub, r, owner), self_sem.at[sub]
                    ).wait()

                @pl.when(jnp.logical_not(is_source))
                def _():
                    arrive(sub, r, owner)
            else:
                arrive(sub, r, owner)
            hand_on(sub, r, owner, s2_send.at[sub, owner, 0], x_row).start()
            hand_on(sub, r, owner, s2_send.at[sub, owner, 1], pair_row).start()
        return run

    def forward_piece(sub):
        def run(owner):
            arrive(sub, x_row, owner)
            hand_on(sub, x_row, owner, fwd_send.at[sub, owner], pair_row).start()
        return run

    def gather(sub):
        for at, offset in enumerate(steps):
            each(offset, own_piece_at(sub, offset))
            if at:
                each(steps[at - 1], forward_piece(sub))
        each(steps[-1], forward_piece(sub))

    def sort_front():
        front_copy.wait()
        for i in range(win_blocks):
            front_sorted[i * BLK:(i + 1) * BLK, :] = picked(
                lambda j: front[j * BLK:(j + 1) * BLK, :], i, front.shape[1]
            )

    def build_window(part):
        for side in range(2):
            take_window(part, n_col - 1, side, False)
        for owner in range(n_col):
            high, low = split(win[part, owner])
            at = owner * width
            rows = slice(part * keep, (part + 1) * keep)
            a_cat[rows, at:at + width] = high
            a_cat[rows, depth + at:depth + at + width] = high
            a_cat[rows, 2 * depth + at:2 * depth + at + width] = low

    tile = 2 * BLK
    tiles = n_row * BLK // tile

    def build_columns(sub):
        for q in (pair_row, (1 - x) * 2 + 1 - k):
            for offset in steps:
                each(offset, lambda owner: arrive(sub, q, owner))
        for owner in range(n_col):
            high, low = split(col[sub, owner])
            at = owner * width
            b_cat[sub, :, at:at + width] = high
            b_cat[sub, :, depth + at:depth + at + width] = low
            b_cat[sub, :, 2 * depth + at:2 * depth + at + width] = high

    def multiply(sub, part):
        into = snd if part == 0 else mine_ref
        for t in range(tiles):
            product = lax.dot_general(
                a_cat[part * keep:(part + 1) * keep, :], b_cat[sub, t * tile:(t + 1) * tile, :],
                (((1,), (1,)), ((), ())), preferred_element_type=F32,
            )
            for b in range(2):
                q = t * 2 + b
                column = (q * subs + sub) * BLK
                into[sub * n_row + q] = (
                    front_sorted[part * keep:(part + 1) * keep, column:column + BLK]
                    - product[:, b * BLK:(b + 1) * BLK]
                )

    def send_sibling(sub):
        for t in range(tiles):
            sibling(sub, t).start()

    def sibling(sub, t):
        blocks = pl.ds(sub * n_row + t * 2, 2)
        return remote(
            snd.at[blocks], got_ref.at[blocks], sib_send.at[sub, t], sib_recv.at[sub, t], other_leaf=sib
        )

    sort_front()
    for sub in range(subs):
        gather(sub)
        if sub == 0:
            build_window(0)
        build_columns(sub)
        multiply(sub, 0)
        send_sibling(sub)
    relay_window(1)
    build_window(1)
    for sub in range(subs):
        multiply(sub, 1)

    for sub in range(subs):
        for t in range(tiles):
            sibling(sub, t).wait()
    other_cols.wait()
    to_relay.wait_send()
    for part in range(2):
        for side in range(2):
            @pl.when(has(side))
            def _():
                pass_window(part, c, side).wait_send()

            for d in range(1, n_col - 1):
                owner = c - d if side == 0 else c + d

                @pl.when(jnp.logical_and(from_left(d) if side == 0 else from_right(d), has(side)))
                def _():
                    pass_window(part, owner, side).wait_send()
    for sub in range(subs):
        for own in (True, False):
            for kk in range(2):
                here, away, stay = scatter(sub, own, kk)

                @pl.when(jnp.logical_not(here))
                def _():
                    away.wait_send()
        for offset in steps:
            def settle(owner):
                hand_on(sub, r, owner, s2_send.at[sub, owner, 0], x_row).wait_send()
                hand_on(sub, r, owner, s2_send.at[sub, owner, 1], pair_row).wait_send()
                hand_on(sub, x_row, owner, fwd_send.at[sub, owner], pair_row).wait_send()

            each(offset, settle)


def merge_kernel(n_row, subs, blocks, own_ref, other_ref, mine_hbm, got_hbm, out_ref, got_ref, mine_sem, got_sem):
    def at(j):
        return (j % subs) * n_row + j // subs

    def spot(maps, j):
        return pl.ds(pl.multiple_of(maps[0, j] * BLK, BLK), BLK)

    def bring(j):
        return pltpu.make_async_copy(got_hbm.at[at(j)], got_ref.at[j], got_sem.at[j])

    def lay(j):
        return pltpu.make_async_copy(mine_hbm.at[at(j)], out_ref.at[:, spot(own_ref, j)], mine_sem.at[j])

    for j in range(blocks):
        lay(j).start()
    for j in range(blocks):
        bring(j).start()
    for j in range(blocks, out_ref.shape[1] // BLK):
        out_ref[:, spot(own_ref, j)] = jnp.zeros((out_ref.shape[0], BLK), F32)
    for j in range(blocks):
        lay(j).wait()
    for j in range(blocks):
        bring(j).wait()
        out_ref[:, spot(other_ref, j)] = out_ref[:, spot(other_ref, j)] + got_ref[j]


def body(sizes, panel, block_mask, front_rest, row_maps, col_maps):
    n_leaf, n_row, n_col = sizes
    local_rows, width = panel.shape
    win_rows, front_cols = front_rest.shape
    keep = win_rows // 2
    blocks = front_cols // BLK
    subs = local_rows // n_row // BLK
    parent_cols = PC // n_col
    win_blocks = win_rows // BLK
    pick = (row_maps == jnp.arange(win_blocks, dtype=row_maps.dtype)[:, None]).astype(F32)
    pick = jnp.broadcast_to(pick.reshape(-1, 1, 1), (win_blocks * win_blocks, 1, front_cols))
    vmem = pl.BlockSpec(memory_space=pltpu.VMEM)
    smem = pl.BlockSpec(memory_space=pltpu.SMEM)
    dma = pltpu.SemaphoreType.DMA
    part = jax.ShapeDtypeStruct((blocks, keep, BLK), F32)
    mine, got, other_cols = pl.pallas_call(
        functools.partial(update_kernel, n_leaf, n_row, n_col),
        out_shape=(part, part, jax.ShapeDtypeStruct(col_maps.shape, col_maps.dtype)),
        in_specs=[vmem] * 4 + [pl.BlockSpec(memory_space=pltpu.HBM)],
        out_specs=(vmem, vmem, vmem),
        scratch_shapes=[
            pltpu.VMEM((local_rows, width), F32),
            pltpu.VMEM((local_rows // 2, width), F32),
            pltpu.VMEM((2, n_col, keep, width), F32),
            pltpu.VMEM((subs, n_col, n_row * BLK, width), F32),
            pltpu.VMEM((win_rows, 3 * n_col * width), BF16),
            pltpu.VMEM((subs, n_row * BLK, 3 * n_col * width), BF16),
            pltpu.VMEM((win_rows, front_cols), F32),
            pltpu.VMEM((win_rows, front_cols), F32),
            pltpu.VMEM((blocks, keep, BLK), F32),
            dma((2, 2, n_col)), dma((2, n_col)),
            dma((1,)), dma((1,)),
            dma((subs, 2, 2)), dma((subs, n_row, n_col)),
            dma((subs, n_col, 2)), dma((subs, n_col)),
            dma((subs, n_row // 2)), dma((subs, n_row // 2)),
            dma((1,)), dma((subs,)), dma((1,)), dma((1,)),
        ],
        compiler_params=pltpu.CompilerParams(
            collective_id=0, has_side_effects=True, vmem_limit_bytes=40 * 1024 * 1024
        ),
        name="update",
    )(pick, block_mask, col_maps, panel, front_rest)
    return pl.pallas_call(
        functools.partial(merge_kernel, n_row, subs, blocks),
        out_shape=jax.ShapeDtypeStruct((keep, parent_cols), F32),
        in_specs=[smem, smem] + [pl.BlockSpec(memory_space=pl.ANY)] * 2,
        out_specs=vmem,
        scratch_shapes=[pltpu.VMEM((blocks, keep, BLK), F32), dma((blocks,)), dma((blocks,))],
        compiler_params=pltpu.CompilerParams(vmem_limit_bytes=8 * 1024 * 1024),
        name="merge",
    )(col_maps, other_cols, mine, got)


def solution(mesh):
    sizes = mesh.shape["leaf"], mesh.shape["row"], mesh.shape["col"]
    return jax.shard_map(
        functools.partial(body, sizes),
        mesh=mesh,
        in_specs=(
            P(("leaf", "row"), "col"),
            P(("leaf", "row"), "col"),
            P(("leaf", "row"), "col"),
            P(("leaf", "row"), None),
            P(("leaf", "col"), None),
        ),
        out_specs=P(("leaf", "row"), "col"),
        check_vma=False,
    )
```

profile of v0, /device:TPU:3, one launch (start us, length us, event | category | flops | bytes accessed | tf_op | source)
XLA Modules:
  0.0 95.7 jit_solution(16086351627073581954)
XLA Ops:
  0.0 0.7 fusion
  0.7 0.1 reshape.20
  0.7 0.8 copy.6.flag_ref
  1.5 0.1 broadcast_in_dim.2.pick_ref
  1.6 0.0 copy-start
  1.6 1.6 %copy-done = f32[512,1024]{1,0:T(8,128)S(1)} copy-done((f32[512,1024]{1,0:T(8,128)S(1)}, f32[512,1024]{1,0:T(8,128)}, u32[]{:S(2)}) %copy-start) | copy-done | bytes 2097176
  3.2 0.0 copy-start.1
  3.2 1.2 %copy-done.1 = f32[1024,256]{1,0:T(8,128)S(1)} copy-done((f32[1024,256]{1,0:T(8,128)S(1)}, f32[1024,256]{1,0:T(8,128)}, u32[]{:S(2)}) %copy-start.1) | copy-done | bytes 1048600
  4.4 0.0 copy-start.2
  4.4 0.7 copy-done.2
  5.1 87.0 %update.1 = (f32[8,256,128]{2,1,0:T(8,128)S(1)}, f32[8,256,128]{2,1,0:T(8,128)S(1)}, s32[1,12]{1,0:T(1,128)S(1)}) custom-call(f32[16,1,1024]{2,1,0:T(1,128)S(1)} %broadcast_in_dim.2.pick_ref, s32[8,2]{1,0:T(8,128)S(1)} %copy.6.flag_ref, s32[1,12]{1,0:T(1,128)S(1)} %copy-done.2, f32[1024,256]{1,0:T(8,128)S(1)} %copy-done.1, f32[512,1024]{1,0:T(8,128)S(1)} %copy-done), custom_call_target="tpu_custom_call" | custom-call | tf_op jit(solution)/shard_map/update/pallas_call | solution.py:387
  92.1 3.6 %merge.1 = f32[256,1536]{1,0:T(8,128)} custom-call(s32[1,12]{1,0:T(1,128)S(1)} %copy-done.2, s32[1,12]{1,0:T(1,128)S(1)} %get-tuple-element.8.other_ref, f32[8,256,128]{2,1,0:T(8,128)S(1)} %get-tuple-element.9.mine_hbm, f32[8,256,128]{2,1,0:T(8,128)S(1)} %get-tuple-element.10.got_hbm), custom_call_target="tpu_custom_call" | custom-call | tf_op jit(solution)/shard_map/merge/pallas_call | solution.py:414
Async XLA Ops:
  1.6 1.6 %copy-start = (f32[512,1024]{1,0:T(8,128)S(1)}, f32[512,1024]{1,0:T(8,128)}, u32[]{:S(2)}) copy-start(f32[512,1024]{1,0:T(8,128)} %front_hbm.1) | copy-start | bytes 6291460
  3.2 1.2 %copy-start.1 = (f32[1024,256]{1,0:T(8,128)S(1)}, f32[1024,256]{1,0:T(8,128)}, u32[]{:S(2)}) copy-start(f32[1024,256]{1,0:T(8,128)} %panel_ref.1) | copy-start | bytes 3145732
  4.4 0.7 copy-start.2
where the time goes:
time: 96 us; the launch traced here: 95.7 us
  Pallas kernels  90.6 us (94%)
  local copies, waits for them, and re-layouts  4.4 us (5%)
    pallas_call x1, Pallas kernels, body(): pl.pallas_call(functools.partial(update_kernel, n_leaf, n_row, n_col), ou...  87 us
    unnamed x7, local copies, waits for them, and re-layouts  4.22 us
    pallas_call x1, Pallas kernels, body(): pl.pallas_call(functools.partial(merge_kernel, n_row, subs, blocks), out_...  3.6 us

commit v1 on v0

v1 whole, which is shorter than its diff:
```python
import functools

import jax
import jax.numpy as jnp
from jax import lax
from jax.experimental import pallas as pl
from jax.experimental.pallas import tpu as pltpu
from jax.sharding import PartitionSpec as P

BLK = 128
PC = 6144
F32 = jnp.float32
BF16 = jnp.bfloat16

LEFT, RIGHT, PAIR, CROSS, DIAG = range(5)
STORE = (0, 1, 6, 7, 2, 4, 3, 5)


def split(value):
    high = value.astype(BF16)
    return high, (value - high.astype(F32)).astype(BF16)


def update_kernel(
    n_leaf, n_row, n_col,
    panel_hbm, mask_hbm, front_hbm, rows_hbm, cols_hbm,
    out_ref,
    big, panel, panel_low, front, a_cat, b_cat, snd, got, mine,
    rows_own, rows_col, rows_other, cols_own, cols_other,
    mask_s, rows_own_s, rows_col_s, rows_other_s, cols_own_s, cols_other_s,
    send, recv, sib_send, sib_recv, map_send, map_recv, loc,
):
    leaf, r, c = lax.axis_index("leaf"), lax.axis_index("row"), lax.axis_index("col")
    x, k = r // 2, r % 2
    sib = lax.rem(leaf + n_leaf // 2, n_leaf)
    upper = leaf // (n_leaf // 2) % 2
    width = panel.shape[2]
    blocks, win_blocks = front.shape[:2]
    half = win_blocks // 2
    keep = half * BLK
    lanes = width // BLK
    parents = out_ref.shape[1] // BLK
    span = 3 * width

    pair_row, x_row, diag_row = x * 2 + 1 - k, (1 - x) * 2 + k, (1 - x) * 2 + 1 - k
    is_o, is_q, is_x, is_d = r == c, pair_row == c, x_row == c, diag_row == c

    def to(row=None, column=None, other_leaf=None):
        return {
            "leaf": leaf if other_leaf is None else other_leaf,
            "row": r if row is None else row,
            "col": c if column is None else column,
        }

    def remote(src, dst, ssem, rsem, where):
        return pltpu.make_async_remote_copy(
            src_ref=src, dst_ref=dst, send_sem=ssem, recv_sem=rsem,
            device_id=where, device_id_type=pl.DeviceIdType.MESH,
        )

    def push(way, src, j, dst):
        where = {
            LEFT: lambda: to(column=c - 1), RIGHT: lambda: to(column=c + 1),
            PAIR: lambda: to(row=pair_row), CROSS: lambda: to(row=x_row), DIAG: lambda: to(row=diag_row),
        }[way]()
        return remote(big.at[src, j], big.at[dst, j], send.at[way, src, j], recv.at[dst, j], where)

    sent, gates = [], []

    def when(cond, run):
        @pl.when(cond())
        def _():
            gates.append(cond)
            run()
            gates.pop()

    def go(way, copy):
        sent.append((way, copy, tuple(gates)))
        push(way, *copy()).start()

    def settle(count):
        for way, copy, conds in sent[:count]:
            def finish():
                push(way, *copy()).wait_send()
            if conds:
                pl.when(both(*[cond() for cond in conds]))(finish)
            else:
                finish()
        del sent[:count]

    def arrive(slot, j):
        push(PAIR, slot, j, slot).wait_recv()

    def both(*conds):
        total = conds[0]
        for cond in conds[1:]:
            total = jnp.logical_and(total, cond)
        return total

    def fetch(src, dst, n):
        return pltpu.make_async_copy(src, dst, loc.at[n])

    get_rows = fetch(rows_hbm, rows_own, 0)
    get_mask = fetch(mask_hbm, mask_s, 1)
    get_win = fetch(panel_hbm.at[pl.ds(0, win_blocks)], panel, 2)
    rest = pl.ds(win_blocks, blocks - win_blocks)
    get_low = fetch(panel_hbm.at[rest], panel_low, 3)
    get_cols = fetch(cols_hbm, cols_own, 4)
    get_front = [
        fetch(front_hbm.at[:, :, pl.ds(m * BLK, BLK)], front.at[m], 5 + m) for m in range(blocks)
    ]
    get_rows.start()
    get_mask.start()
    get_win.start()
    get_low.start()
    get_cols.start()
    for copy in get_front:
        copy.start()

    barrier = pltpu.get_barrier_semaphore()

    def greet(where):
        pl.semaphore_signal(barrier, inc=1, device_id=where, device_id_type=pl.DeviceIdType.MESH)

    has_left, has_right = c >= 1, c + 1 < n_col

    @pl.when(has_left)
    def _():
        greet(to(column=c - 1))

    @pl.when(has_right)
    def _():
        greet(to(column=c + 1))

    greet(to(row=x_row))
    greet(to(row=diag_row))
    greet(to(other_leaf=sib))
    greet(to(row=pair_row))

    first_kept, first_sent = upper * half, (1 - upper) * half
    order_own = [first_sent + i for i in range(half)] + [first_kept + i for i in range(half)]
    order_other = [first_kept + i for i in range(half)] + [first_sent + i for i in range(half)]

    def place(rows_s, parent):
        at = jnp.int32(0)
        for m in range(1, win_blocks):
            at = jnp.where(rows_s[0, m] == parent, jnp.int32(m), at)
        return at

    def pick(values, at):
        total = jnp.int32(0)
        for m, value in enumerate(values):
            total = total + jnp.where(at == m, value, jnp.int32(0))
        return total

    get_rows.wait()
    own_rows = fetch(rows_own, rows_own_s, 0)
    own_rows.start()
    get_mask.wait()
    own_rows.wait()
    natural = [place(rows_own_s, parent) for parent in order_own]

    def window_base(column):
        return jnp.where(r == column, 0, blocks)

    win_at = window_base(c)
    low_at = jnp.where(is_o, win_blocks, 2 * blocks)

    get_win.wait()
    for b in range(win_blocks):
        block = panel[natural[b]]
        for h in range(lanes):
            cut = slice(h * BLK, (h + 1) * BLK)
            flag = pick([mask_s[h, m] for m in range(win_blocks)], natural[b]).astype(F32)
            big[win_at + b, c, :, cut] = block[:, cut] * flag
    get_low.wait()
    for b in range(win_blocks):
        at = win_blocks + b
        for h in range(lanes):
            cut = slice(h * BLK, (h + 1) * BLK)
            big[low_at + b, c, :, cut] = panel_low[b, :, cut] * mask_s[h, at].astype(F32)

    pl.semaphore_wait(barrier, 4 + has_left.astype(jnp.int32) + has_right.astype(jnp.int32))

    transit = blocks + win_blocks

    def goal(s):
        return pair_row if s < 2 else (1 - x) * 2 + (s - 2)

    def low_slot(s, column):
        block = s if s < 2 else 2 + k
        return jnp.where(goal(s) == column, win_blocks + block, transit + s)

    def has(side):
        return has_right if side else has_left

    def next_of(side):
        return c + 1 if side else c - 1

    def from_at(side, d):
        return c - d if side else c + d

    def there(side, d):
        return from_at(side, d) >= 0 if side else from_at(side, d) < n_col

    def window_on(b, d, side):
        when(lambda: has(side), lambda: go(
            RIGHT if side else LEFT,
            lambda: (win_at + b, from_at(side, d), window_base(next_of(side)) + b),
        ))

    def hand_out(slot, j):
        for way in (CROSS, PAIR):
            go(way, lambda: (slot(), j(), slot()))

    def take_window(b, d):
        for side in (0, 1):
            def run(side=side):
                arrive(win_at + b, from_at(side, d))
                window_on(b, d, side)
                when(lambda: is_o, lambda: hand_out(lambda: b, lambda: from_at(side, d)))
            when(lambda side=side: there(side, d), run)

    def ahead(s, side):
        return goal(s) > c if side else goal(s) < c

    def low_on(s, d, side):
        go(RIGHT if side else LEFT, lambda: (low_slot(s, c), from_at(side, d), low_slot(s, next_of(side))))

    def take_low(s, d):
        for side in (0, 1):
            def wanted(side=side):
                return both(there(side, d), jnp.logical_or(ahead(s, side), goal(s) == c))

            def run(side=side):
                arrive(low_slot(s, c), from_at(side, d))
                when(lambda: ahead(s, side), lambda: low_on(s, d, side))
                when(lambda: goal(s) == c, lambda: hand_out(lambda: low_slot(s, c), lambda: from_at(side, d)))
            when(wanted, run)

    def own_low(side):
        for s in LOW:
            def run(s=s):
                arrive(transit + s, c)
                low_on(s, 0, side)
            when(lambda s=s: ahead(s, side), run)

    LOW = (2, 3, 0, 1)

    def not_o():
        return jnp.logical_not(is_o)

    def owner():
        return is_o

    def inner():
        return both(has_left, has_right)

    def outer():
        return jnp.logical_not(inner())

    def scatter():
        go(CROSS, lambda: (low_at + 2 + k, c, transit + 2 + k))
        go(DIAG, lambda: (low_at + 3 - k, c, transit + 2 + k))
        for s in range(2):
            go(PAIR, lambda s=s: (low_at + s, c, transit + s))

    def spread(slots):
        for slot in slots:
            hand_out(lambda slot=slot: slot, lambda: c)

    def at_source(side):
        return c == 0 if side else c == n_col - 1

    def own_late(side):
        for b in range(half, win_blocks):
            window_on(b, 0, side)

    def map_copy(src, dst, n, where, arrived=None):
        return remote(src, dst, map_send.at[n], map_recv.at[n if arrived is None else arrived], where)

    get_cols.wait()
    to_sib_cols = map_copy(cols_own, cols_other, 0, to(other_leaf=sib))
    to_sib_cols.start()
    rows_cross = map_copy(rows_own, rows_col, 1, to(row=x_row))
    rows_pair = map_copy(rows_own, rows_col, 2, to(row=pair_row), 1)
    rows_pass = map_copy(rows_col, rows_col, 2, to(row=pair_row), 1)
    rows_stay = fetch(rows_own, rows_col, 0)
    to_sib_rows = map_copy(rows_col, rows_other, 3, to(other_leaf=sib))

    def rows_from_owner():
        rows_cross.start()
        rows_pair.start()
        rows_stay.start()

    when(owner, rows_from_owner)

    def by_cross(slot, j):
        if slot < win_blocks:
            other = is_x
        elif slot < win_blocks + 2:
            other = is_d
        else:
            other = both(k == slot - win_blocks - 2, jnp.logical_or(is_o, is_q))
        return jnp.where(c == j, is_x, other)

    def by_pair(slot, j):
        if slot < win_blocks:
            other = jnp.logical_or(is_q, is_d)
        elif slot < win_blocks + 2:
            other = jnp.logical_or(is_o, is_x)
        else:
            other = k != slot - win_blocks - 2
        return jnp.where(c == j, jnp.logical_or(is_q, is_d), other)

    def collect(slots):
        for slot in slots:
            for j in range(n_col):
                def run(slot=slot, j=j):
                    arrive(slot, j)
                    go(PAIR, lambda: (slot, j, slot))
                when(lambda slot=slot, j=j: by_cross(slot, j), run)
        for slot in slots:
            for j in range(n_col):
                when(lambda slot=slot, j=j: by_pair(slot, j), lambda: arrive(slot, j))

    def lay_rows(b):
        rows = slice(b * BLK, (b + 1) * BLK)
        for j in range(n_col):
            high, low = split(big[win_at + b, j])
            at = j * span
            a_cat[rows, at:at + width] = high
            a_cat[rows, at + width:at + 2 * width] = high
            a_cat[rows, at + 2 * width:at + span] = low

    def lay_columns(slot):
        rows = slice(STORE.index(slot) * BLK, (STORE.index(slot) + 1) * BLK)
        for j in range(n_col):
            high, low = split(big[slot, j])
            at = j * span
            b_cat[rows, at:at + width] = high
            b_cat[rows, at + width:at + 2 * width] = low
            b_cat[rows, at + 2 * width:at + span] = high

    def multiply(group, part):
        product = lax.dot_general(
            a_cat[part * keep:(part + 1) * keep, :], b_cat[group * 2 * BLK:(group + 1) * 2 * BLK, :],
            (((1,), (1,)), ((), ())), preferred_element_type=F32,
        )
        into = mine if part else snd
        for i in range(2):
            slot = STORE[group * 2 + i]
            column = natural_col[slot] if slot < win_blocks else slot
            for b in range(half):
                into[slot, b * BLK:(b + 1) * BLK, :] = (
                    front[column, natural[part * half + b]] - product[b * BLK:(b + 1) * BLK, i * BLK:(i + 1) * BLK]
                )

    def sibling(slot):
        return remote(snd.at[slot], got.at[slot], sib_send.at[slot], sib_recv.at[slot], to(other_leaf=sib))

    def group_out(group):
        slots = STORE[group * 2:group * 2 + 2]
        for slot in slots:
            lay_columns(slot)
        multiply(group, 0)
        for slot in slots:
            sibling(slot).start()

    def late(b):
        for d in range(1, n_col):
            take_window(b, d)

    def maps_in():
        when(owner, lambda: rows_stay.wait())
        when(not_o, lambda: rows_cross.wait_recv())
        when(lambda: is_x, lambda: rows_pass.start())
        to_sib_rows.start()
        to_col_s = fetch(rows_col, rows_col_s, 0)
        to_col_s.start()
        to_col_s.wait()

    def first_out():
        collect(STORE[:2])
        for b in range(half):
            lay_rows(b)
        for copy in get_front:
            copy.wait()
        group_out(0)

    def middle_inner():
        for d in range(1, n_col):
            for s in LOW:
                take_low(s, d)
        for side in (0, 1):
            when(lambda side=side: jnp.logical_not(at_source(side)), functools.partial(own_late, side))
        first_out()
        late(half)
        collect(STORE[2:4])
        group_out(1)
        collect(STORE[4:6])
        group_out(2)
        late(half + 1)
        collect(STORE[6:])
        group_out(3)

    def middle_outer():
        first_out()
        for s in LOW[:3]:
            for d in range(1, n_col):
                take_low(s, d)
        for side in (0, 1):
            when(lambda side=side: jnp.logical_not(at_source(side)), functools.partial(own_late, side))
        when(owner, functools.partial(late, half))
        collect(STORE[2:4])
        group_out(1)
        for d in range(1, n_col):
            take_low(LOW[3], d)
        collect(STORE[4:6])
        group_out(2)
        when(owner, functools.partial(late, half + 1))
        collect(STORE[6:])
        group_out(3)
        for b in range(half, win_blocks):
            when(not_o, functools.partial(late, b))

    for b in range(half):
        for side in (0, 1):
            window_on(b, 0, side)
    when(not_o, scatter)
    for side in (0, 1):
        def source(side=side):
            own_low(side)
            own_late(side)
        when(lambda side=side: at_source(side), source)

    SPREAD = (range(half), range(win_blocks, blocks), range(half, win_blocks))
    for d in range(1, n_col):
        for b in range(half):
            take_window(b, d)
        when(owner, functools.partial(spread, SPREAD[d - 1]))
        for side in (0, 1):
            last = 0 if side else n_col - 1
            when(lambda side=side, d=d, last=last: from_at(side, d) == last, functools.partial(own_low, side))

    maps_in()
    natural_col = [place(rows_col_s, parent) for parent in order_own]
    when(inner, middle_inner)
    when(outer, middle_outer)
    for b in range(half, win_blocks):
        lay_rows(b)
    for group in range(blocks // 2):
        multiply(group, 1)
    settle(len(sent))

    to_sib_cols.wait_recv()
    to_sib_rows.wait_recv()
    to_own = fetch(cols_own, cols_own_s, 1)
    to_other = fetch(cols_other, cols_other_s, 2)
    to_rows = fetch(rows_other, rows_other_s, 3)
    to_own.start()
    to_other.start()
    to_rows.start()
    to_own.wait()
    to_other.wait()
    to_rows.wait()
    natural_other = [place(rows_other_s, parent) for parent in order_other]

    def spots(cols_s, naturals):
        values = [cols_s[0, m] for m in range(blocks)]
        return [pick(values[:win_blocks], naturals[o]) if o < win_blocks else values[o] for o in range(blocks)]

    spot_own, spot_other = spots(cols_own_s, natural_col), spots(cols_other_s, natural_other)

    for o in range(blocks):
        sibling(o).wait_recv()
    for t in range(parents):
        total = None
        for spot, held in ((spot_own, mine), (spot_other, got)):
            at, found = jnp.int32(0), jnp.int32(0)
            for o in range(blocks):
                hit = spot[o] == t
                at, found = jnp.where(hit, jnp.int32(o), at), jnp.where(hit, jnp.int32(1), found)
            term = held[at] * found.astype(F32)
            total = term if total is None else total + term
        out_ref[:, t * BLK:(t + 1) * BLK] = total

    for o in range(blocks):
        sibling(o).wait_send()
    to_sib_cols.wait_send()
    to_sib_rows.wait_send()
    when(owner, lambda: rows_cross.wait_send())
    when(owner, lambda: rows_pair.wait_send())
    when(lambda: is_x, lambda: rows_pass.wait_send())


def body(sizes, panel, block_mask, front_rest, row_maps, col_maps):
    n_leaf, n_row, n_col = sizes
    local_rows, width = panel.shape
    win_rows, front_cols = front_rest.shape
    keep = win_rows // 2
    blocks = front_cols // BLK
    win_blocks = win_rows // BLK
    parent_cols = PC // n_col
    any_space = pl.BlockSpec(memory_space=pl.ANY)
    dma = pltpu.SemaphoreType.DMA
    slots = 2 * blocks + win_blocks
    rows_type, cols_type = row_maps.dtype, col_maps.dtype
    return pl.pallas_call(
        functools.partial(update_kernel, n_leaf, n_row, n_col),
        out_shape=jax.ShapeDtypeStruct((keep, parent_cols), F32),
        in_specs=[any_space] * 5,
        out_specs=pl.BlockSpec(memory_space=pltpu.VMEM),
        scratch_shapes=[
            pltpu.VMEM((slots, n_col, BLK, width), F32),
            pltpu.VMEM((win_blocks, BLK, width), F32),
            pltpu.VMEM((blocks - win_blocks, BLK, width), F32),
            pltpu.VMEM((blocks, win_blocks, BLK, BLK), F32),
            pltpu.VMEM((win_rows, 3 * n_col * width), BF16),
            pltpu.VMEM((blocks * BLK, 3 * n_col * width), BF16),
            pltpu.VMEM((blocks, keep, BLK), F32),
            pltpu.VMEM((blocks, keep, BLK), F32),
            pltpu.VMEM((blocks, keep, BLK), F32),
            pltpu.VMEM(row_maps.shape, rows_type), pltpu.VMEM(row_maps.shape, rows_type),
            pltpu.VMEM(row_maps.shape, rows_type),
            pltpu.VMEM(col_maps.shape, cols_type), pltpu.VMEM(col_maps.shape, cols_type),
            pltpu.SMEM(block_mask.shape[::-1], block_mask.dtype),
            pltpu.SMEM(row_maps.shape, rows_type), pltpu.SMEM(row_maps.shape, rows_type),
            pltpu.SMEM(row_maps.shape, rows_type),
            pltpu.SMEM(col_maps.shape, cols_type), pltpu.SMEM(col_maps.shape, cols_type),
            dma((5, slots, n_col)), dma((slots, n_col)),
            dma((blocks,)), dma((blocks,)), dma((4,)), dma((4,)), dma((5 + blocks,)),
        ],
        compiler_params=pltpu.CompilerParams(
            collective_id=0, has_side_effects=True, vmem_limit_bytes=60 * 1024 * 1024
        ),
        name="update",
    )(
        panel.reshape(local_rows // BLK, BLK, width), block_mask.T,
        front_rest.reshape(win_blocks, BLK, front_cols), row_maps, col_maps,
    )


def solution(mesh):
    sizes = mesh.shape["leaf"], mesh.shape["row"], mesh.shape["col"]
    return jax.shard_map(
        functools.partial(body, sizes),
        mesh=mesh,
        in_specs=(
            P(("leaf", "row"), "col"),
            P(("leaf", "row"), "col"),
            P(("leaf", "row"), "col"),
            P(("leaf", "row"), None),
            P(("leaf", "col"), None),
        ),
        out_specs=P(("leaf", "row"), "col"),
        check_vma=False,
    )
```

time: 96 us -> 75.2 us (0.78)
  Pallas kernels: 90.6 us -> 72.4 us
  local copies, waits for them, and re-layouts: 4.4 us -> 2.66 us
    pallas_call x1, Pallas kernels: 87 us -> 72.4 us  [body(): pl.pallas_call(functools.partial(update_kernel, n_leaf, n_row, n_col), ou...]
    pallas_call x1 -> x0, Pallas kernels: 3.6 us -> none  [body(): pl.pallas_call(functools.partial(merge_kernel, n_row, subs, blocks), out_...]
    unnamed x7 -> x1, local copies, waits for them, and re-layouts: 4.22 us -> 2.66 us
where the time goes in v1:
time: 75.2 us; the launch traced here: 75.1 us
  Pallas kernels  72.4 us (96%)
  local copies, waits for them, and re-layouts  2.66 us (4%)
    pallas_call x1, Pallas kernels, body(): pl.pallas_call(functools.partial(update_kernel, n_leaf, n_row, n_col), ou...  72.4 us
    unnamed x1, local copies, waits for them, and re-layouts  2.66 us

profile of v1, /device:TPU:3, one launch (start us, length us, event | category | flops | bytes accessed | tf_op | source)
XLA Modules:
  0.0 75.1 jit_solution(2748837168310092272)
XLA Ops:
  0.0 72.4 %update.1 = f32[256,1536]{1,0:T(8,128)} custom-call(f32[8,128,256]{2,1,0:T(8,128)} %bitcast.4, s32[2,8]{1,0:T(2,128)} %bitcast.5, f32[4,128,1024]{2,1,0:T(8,128)} %bitcast.3, s32[1,4]{1,0:T(1,128)} %rows_hbm.1, s32[1,12]{1,0:T(1,128)} %cols_hbm.1), custom_call_target="tpu_custom_call" | custom-call | tf_op jit(solution)/shard_map/update/pallas_call | solution.py:509
  72.4 2.7 %copy.7 = f32[256,1536]{1,0:T(8,128)} copy(f32[256,1536]{1,0:T(8,128)} %update.1) | data formatting | bytes 3145728

commit v2 on v1

--- a/solution.py
+++ b/solution.py
@@ -13,7 +13,19 @@
 BF16 = jnp.bfloat16
 
 LEFT, RIGHT, PAIR, CROSS, DIAG = range(5)
-STORE = (0, 1, 6, 7, 2, 4, 3, 5)
+GROUPS = ((0, 1), (6, 7), (2, 4), (3,), (5,))
+STORE = tuple(slot for group in GROUPS for slot in group)
+INNER = (
+    "S7", "S1", "A1", "S0", "A2", "S2", "S6", "S3", "S4", "S5", "x01", "x21",
+    "x31", "M", "x02", "x11", "x22", "x32", "x12", "L", "G0", "w21", "G1", "w22",
+    "w31", "w32o", "G4", "G2", "G3", "w32n",
+)
+OUTER = (
+    "S3", "S2", "x21", "x31", "M", "x22", "S6", "S0", "S7", "A2", "A1", "x23",
+    "A3", "S1", "x03", "x32", "x02", "G0", "S5", "S4", "L", "w21o", "x01", "x33",
+    "x11", "G1", "w22o", "w23o", "w22n", "w31o", "x13", "x12", "G2", "G4", "w31n", "w32o",
+    "w32n", "w33o", "w21n", "G3", "w33n", "w23n",
+)
 
 
 def split(value):
@@ -78,15 +90,14 @@
         sent.append((way, copy, tuple(gates)))
         push(way, *copy()).start()
 
-    def settle(count):
-        for way, copy, conds in sent[:count]:
+    def settle(copies, depth):
+        for way, copy, conds in copies:
             def finish():
                 push(way, *copy()).wait_send()
-            if conds:
-                pl.when(both(*[cond() for cond in conds]))(finish)
+            if conds[depth:]:
+                pl.when(both(*[cond() for cond in conds[depth:]]))(finish)
             else:
                 finish()
-        del sent[:count]
 
     def arrive(slot, j):
         push(PAIR, slot, j, slot).wait_recv()
@@ -101,6 +112,7 @@
         return pltpu.make_async_copy(src, dst, loc.at[n])
 
     get_rows = fetch(rows_hbm, rows_own, 0)
+    get_rows_s = fetch(rows_hbm, rows_own_s, 5 + blocks)
     get_mask = fetch(mask_hbm, mask_s, 1)
     get_win = fetch(panel_hbm.at[pl.ds(0, win_blocks)], panel, 2)
     rest = pl.ds(win_blocks, blocks - win_blocks)
@@ -109,10 +121,11 @@
     get_front = [
         fetch(front_hbm.at[:, :, pl.ds(m * BLK, BLK)], front.at[m], 5 + m) for m in range(blocks)
     ]
-    get_rows.start()
+    get_rows_s.start()
     get_mask.start()
     get_win.start()
     get_low.start()
+    get_rows.start()
     get_cols.start()
     for copy in get_front:
         copy.start()
@@ -153,11 +166,8 @@
             total = total + jnp.where(at == m, value, jnp.int32(0))
         return total
 
-    get_rows.wait()
-    own_rows = fetch(rows_own, rows_own_s, 0)
-    own_rows.start()
     get_mask.wait()
-    own_rows.wait()
+    get_rows_s.wait()
     natural = [place(rows_own_s, parent) for parent in order_own]
 
     def window_base(column):
@@ -259,6 +269,12 @@
     def outer():
         return jnp.logical_not(inner())
 
+    def near():
+        return jnp.logical_or(is_o, is_q)
+
+    def far():
+        return jnp.logical_not(near())
+
     def scatter():
         go(CROSS, lambda: (low_at + 2 + k, c, transit + 2 + k))
         go(DIAG, lambda: (low_at + 3 - k, c, transit + 2 + k))
@@ -279,6 +295,7 @@
     def map_copy(src, dst, n, where, arrived=None):
         return remote(src, dst, map_send.at[n], map_recv.at[n if arrived is None else arrived], where)
 
+    get_rows.wait()
     get_cols.wait()
     to_sib_cols = map_copy(cols_own, cols_other, 0, to(other_leaf=sib))
     to_sib_cols.start()
@@ -342,15 +359,15 @@
             b_cat[rows, at + width:at + 2 * width] = low
             b_cat[rows, at + 2 * width:at + span] = high
 
-    def multiply(group, part):
+    def multiply(slots, part):
+        first = STORE.index(slots[0])
         product = lax.dot_general(
-            a_cat[part * keep:(part + 1) * keep, :], b_cat[group * 2 * BLK:(group + 1) * 2 * BLK, :],
+            a_cat[part * keep:(part + 1) * keep, :], b_cat[first * BLK:(first + len(slots)) * BLK, :],
             (((1,), (1,)), ((), ())), preferred_element_type=F32,
         )
         into = mine if part else snd
-        for i in range(2):
-            slot = STORE[group * 2 + i]
-            column = natural_col[slot] if slot < win_blocks else slot
+        for i, slot in enumerate(slots):
+            column = place(rows_col_s, order_own[slot]) if slot < win_blocks else slot
             for b in range(half):
                 into[slot, b * BLK:(b + 1) * BLK, :] = (
                     front[column, natural[part * half + b]] - product[b * BLK:(b + 1) * BLK, i * BLK:(i + 1) * BLK]
@@ -360,16 +377,18 @@
         return remote(snd.at[slot], got.at[slot], sib_send.at[slot], sib_recv.at[slot], to(other_leaf=sib))
 
     def group_out(group):
-        slots = STORE[group * 2:group * 2 + 2]
+        slots = GROUPS[group]
+        collect(slots)
+        if group == 0:
+            for b in range(half):
+                lay_rows(b)
+            for copy in get_front:
+                copy.wait()
         for slot in slots:
             lay_columns(slot)
-        multiply(group, 0)
+        multiply(slots, 0)
         for slot in slots:
             sibling(slot).start()
-
-    def late(b):
-        for d in range(1, n_col):
-            take_window(b, d)
 
     def maps_in():
         when(owner, lambda: rows_stay.wait())
@@ -380,49 +399,41 @@
         to_col_s.start()
         to_col_s.wait()
 
-    def first_out():
-        collect(STORE[:2])
+    def windows(d):
         for b in range(half):
-            lay_rows(b)
-        for copy in get_front:
-            copy.wait()
-        group_out(0)
-
-    def middle_inner():
-        for d in range(1, n_col):
-            for s in LOW:
-                take_low(s, d)
+            take_window(b, d)
+        for side in (0, 1):
+            last = 0 if side else n_col - 1
+            when(lambda side=side, last=last: from_at(side, d) == last, functools.partial(own_low, side))
+
+    def own_rest():
         for side in (0, 1):
             when(lambda side=side: jnp.logical_not(at_source(side)), functools.partial(own_late, side))
-        first_out()
-        late(half)
-        collect(STORE[2:4])
-        group_out(1)
-        collect(STORE[4:6])
-        group_out(2)
-        late(half + 1)
-        collect(STORE[6:])
-        group_out(3)
-
-    def middle_outer():
-        first_out()
-        for s in LOW[:3]:
-            for d in range(1, n_col):
-                take_low(s, d)
-        for side in (0, 1):
-            when(lambda side=side: jnp.logical_not(at_source(side)), functools.partial(own_late, side))
-        when(owner, functools.partial(late, half))
-        collect(STORE[2:4])
-        group_out(1)
-        for d in range(1, n_col):
-            take_low(LOW[3], d)
-        collect(STORE[4:6])
-        group_out(2)
-        when(owner, functools.partial(late, half + 1))
-        collect(STORE[6:])
-        group_out(3)
-        for b in range(half, win_blocks):
-            when(not_o, functools.partial(late, b))
+
+    def step(token):
+        kind, rest = token[0], token[1:]
+        if kind == "A":
+            windows(int(rest))
+        elif kind == "S":
+            when(owner, functools.partial(spread, (int(rest),)))
+        elif kind == "M":
+            maps_in()
+        elif kind == "L":
+            own_rest()
+        elif kind == "G":
+            group_out(int(rest))
+        elif kind == "x":
+            take_low(int(rest[0]), int(rest[1]))
+        else:
+            run = functools.partial(take_window, int(rest[0]), int(rest[1]))
+            if rest[2:]:
+                when(owner if rest[2:] == "o" else not_o, run)
+            else:
+                run()
+
+    def follow(tokens):
+        for token in tokens:
+            step(token)
 
     for b in range(half):
         for side in (0, 1):
@@ -434,24 +445,19 @@
             own_late(side)
         when(lambda side=side: at_source(side), source)
 
-    SPREAD = (range(half), range(win_blocks, blocks), range(half, win_blocks))
-    for d in range(1, n_col):
-        for b in range(half):
-            take_window(b, d)
-        when(owner, functools.partial(spread, SPREAD[d - 1]))
-        for side in (0, 1):
-            last = 0 if side else n_col - 1
-            when(lambda side=side, d=d, last=last: from_at(side, d) == last, functools.partial(own_low, side))
-
-    maps_in()
-    natural_col = [place(rows_col_s, parent) for parent in order_own]
-    when(inner, middle_inner)
-    when(outer, middle_outer)
+    first = len(sent)
+    parts = []
+    for mine_too, tokens in ((inner, INNER), (outer, OUTER)):
+        before = len(sent)
+        when(mine_too, functools.partial(follow, tokens))
+        parts.append((mine_too, sent[before:]))
     for b in range(half, win_blocks):
         lay_rows(b)
-    for group in range(blocks // 2):
-        multiply(group, 1)
-    settle(len(sent))
+    for slots in GROUPS:
+        multiply(slots, 1)
+    for mine_too, copies in parts:
+        when(mine_too, functools.partial(settle, copies, 1))
+    settle(sent[:first], 0)
 
     to_sib_cols.wait_recv()
     to_sib_rows.wait_recv()
@@ -464,6 +470,7 @@
     to_own.wait()
     to_other.wait()
     to_rows.wait()
+    natural_col = [place(rows_col_s, parent) for parent in order_own]
     natural_other = [place(rows_other_s, parent) for parent in order_other]
 
     def spots(cols_s, naturals):
@@ -472,18 +479,18 @@
 
     spot_own, spot_other = spots(cols_own_s, natural_col), spots(cols_other_s, natural_other)
 
+    def source_of(spot, t):
+        at, found = jnp.int32(0), jnp.int32(0)
+        for o in range(blocks):
+            hit = spot[o] == t
+            at, found = jnp.where(hit, jnp.int32(o), at), jnp.where(hit, jnp.int32(1), found)
+        return at, found.astype(F32)
+
+    sources = [(source_of(spot_own, t), source_of(spot_other, t)) for t in range(parents)]
     for o in range(blocks):
         sibling(o).wait_recv()
-    for t in range(parents):
-        total = None
-        for spot, held in ((spot_own, mine), (spot_other, got)):
-            at, found = jnp.int32(0), jnp.int32(0)
-            for o in range(blocks):
-                hit = spot[o] == t
-                at, found = jnp.where(hit, jnp.int32(o), at), jnp.where(hit, jnp.int32(1), found)
-            term = held[at] * found.astype(F32)
-            total = term if total is None else total + term
-        out_ref[:, t * BLK:(t + 1) * BLK] = total
+    for t, ((at, found), (at_got, found_got)) in enumerate(sources):
+        out_ref[:, t * BLK:(t + 1) * BLK] = mine[at] * found + got[at_got] * found_got
 
     for o in range(blocks):
         sibling(o).wait_send()
@@ -529,16 +536,16 @@
             pltpu.SMEM(row_maps.shape, rows_type),
             pltpu.SMEM(col_maps.shape, cols_type), pltpu.SMEM(col_maps.shape, cols_type),
             dma((5, slots, n_col)), dma((slots, n_col)),
-            dma((blocks,)), dma((blocks,)), dma((4,)), dma((4,)), dma((5 + blocks,)),
+            dma((blocks,)), dma((blocks,)), dma((4,)), dma((4,)), dma((6 + blocks,)),
         ],
         compiler_params=pltpu.CompilerParams(
-            collective_id=0, has_side_effects=True, vmem_limit_bytes=60 * 1024 * 1024
+            collective_id=0, has_side_effects=True, vmem_limit_bytes=40 * 1024 * 1024
         ),
         name="update",
-    )(
+    )(*[pltpu.with_memory_space_constraint(value, pltpu.HBM) for value in (
         panel.reshape(local_rows // BLK, BLK, width), block_mask.T,
         front_rest.reshape(win_blocks, BLK, front_cols), row_maps, col_maps,
-    )
+    )])
 
 
 def solution(mesh):

time: 75.2 us -> 67.7 us (0.900)
  Pallas kernels: 72.4 us -> 66.4 us
  local copies, waits for them, and re-layouts: 2.66 us -> 1.15 us
    pallas_call x1, Pallas kernels: 72.4 us -> 66.4 us  [body(): pl.pallas_call(functools.partial(update_kernel, n_leaf, n_row, n_col), ou...]
    unnamed x1, local copies, waits for them, and re-layouts: 2.66 us -> 1.15 us
where the time goes in v2:
time: 67.7 us; the launch traced here: 67.5 us
  Pallas kernels  66.4 us (98%)
  local copies, waits for them, and re-layouts  1.15 us (2%)
    pallas_call x1, Pallas kernels, body(): pl.pallas_call(functools.partial(update_kernel, n_leaf, n_row, n_col), ou...  66.4 us

profile of v2, /device:TPU:3, one launch (start us, length us, event | category | flops | bytes accessed | tf_op | source)
XLA Modules:
  0.0 67.5 jit_solution(6324795834297144379)
XLA Ops:
  0.0 66.4 %update.1 = f32[256,1536]{1,0:T(8,128)S(1)} custom-call(f32[8,128,256]{2,1,0:T(8,128)} %bitcast.4, s32[2,8]{1,0:T(2,128)} %bitcast.5, f32[4,128,1024]{2,1,0:T(8,128)} %bitcast.3, s32[1,4]{1,0:T(1,128)} %rows_hbm.1, s32[1,12]{1,0:T(1,128)} %cols_hbm.1), custom_call_target="tpu_custom_call" | custom-call | tf_op jit(solution)/shard_map/update/pallas_call | solution.py:516
  66.4 1.1 %copy.7 = f32[256,1536]{1,0:T(8,128)} copy(f32[256,1536]{1,0:T(8,128)S(1)} %update.1) | data formatting | bytes 3145728

commit v3 on v2

--- a/solution.py
+++ b/solution.py
@@ -16,15 +16,15 @@
 GROUPS = ((0, 1), (6, 7), (2, 4), (3,), (5,))
 STORE = tuple(slot for group in GROUPS for slot in group)
 INNER = (
-    "S7", "S1", "A1", "S0", "A2", "S2", "S6", "S3", "S4", "S5", "x01", "x21",
-    "x31", "M", "x02", "x11", "x22", "x32", "x12", "L", "G0", "w21", "G1", "w22",
-    "w31", "w32o", "G4", "G2", "G3", "w32n",
+    "S5", "S1", "M", "S3", "A1", "S0", "A2", "S6", "x01", "S7", "S2", "x21",
+    "x31", "x02", "x11", "G0", "x22", "L", "x12", "x32", "w21", "G1", "w22", "S4",
+    "w32o", "w31", "G4", "G2", "w32n", "G3",
 )
 OUTER = (
-    "S3", "S2", "x21", "x31", "M", "x22", "S6", "S0", "S7", "A2", "A1", "x23",
-    "A3", "S1", "x03", "x32", "x02", "G0", "S5", "S4", "L", "w21o", "x01", "x33",
-    "x11", "G1", "w22o", "w23o", "w22n", "w31o", "x13", "x12", "G2", "G4", "w31n", "w32o",
-    "w32n", "w33o", "w21n", "G3", "w33n", "w23n",
+    "x21", "S3", "S1", "S7", "A2", "x31", "x32", "x22", "S0", "A1", "A3", "S2",
+    "S5", "M", "S4", "S6", "x03", "L", "x23", "x01", "G0", "x33", "x02", "w22o",
+    "x11", "w21o", "G1", "w23o", "G2", "w21n", "x12", "x13", "w23n", "w32o", "w33o", "w32n",
+    "w31o", "G4", "G3", "w31n", "w33n", "w22n",
 )
 
 

time: 67.7 us -> 67.3 us (level); the launches traced: 67.5 us -> 66 us
  Pallas kernels: 66.4 us -> 64.9 us
    pallas_call x1, Pallas kernels: 66.4 us -> 64.9 us  [body(): pl.pallas_call(functools.partial(update_kernel, n_leaf, n_row, n_col), ou...]
where the time goes in v3:
time: 67.3 us; the launch traced here: 66 us
  Pallas kernels  64.9 us (96%)
  local copies, waits for them, and re-layouts  1.15 us (2%)
    pallas_call x1, Pallas kernels, body(): pl.pallas_call(functools.partial(update_kernel, n_leaf, n_row, n_col), ou...  64.9 us

profile of v3, /device:TPU:3, one launch (start us, length us, event | category | flops | bytes accessed | tf_op | source)
XLA Modules:
  0.0 66.0 jit_solution(1497528332180440332)
XLA Ops:
  0.0 64.9 %update.1 = f32[256,1536]{1,0:T(8,128)S(1)} custom-call(f32[8,128,256]{2,1,0:T(8,128)} %bitcast.4, s32[2,8]{1,0:T(2,128)} %bitcast.5, f32[4,128,1024]{2,1,0:T(8,128)} %bitcast.3, s32[1,4]{1,0:T(1,128)} %rows_hbm.1, s32[1,12]{1,0:T(1,128)} %cols_hbm.1), custom_call_target="tpu_custom_call" | custom-call | tf_op jit(solution)/shard_map/update/pallas_call | solution.py:516
  64.9 1.1 %copy.7 = f32[256,1536]{1,0:T(8,128)} copy(f32[256,1536]{1,0:T(8,128)S(1)} %update.1) | data formatting | bytes 3145728
